TPU v7x, 32 devices: a whole 2x2x4 slice. The times are simulated.
32 devices in a mesh: groups: 2 (over x), tensor: 4 (over y, core), dp: 4 (over z).
Axes of the slice: x: 2, y: 2, z: 4, core: 2. Of those that a mesh axis runs over, the one named last changes fastest.
Arguments:
- hidden_in: bfloat16 [1024, 8192], P(('groups', 'dp'), 'tensor'), parts along dimension 0, may hold values from -6 to 6
- out_grad: bfloat16 [1024, 8192], P(('groups', 'dp'), 'tensor'), parts along dimension 0, may hold values from -6 to 6
- w_gate_up: bfloat16 [2, 28672, 8192], P(None, ('tensor', 'dp')), may hold values from -0.0625 to 0.0625
- w_down: bfloat16 [28672, 8192], P(('tensor', 'dp')), may hold values from -0.03125 to 0.03125
- feat_proj: bfloat16 [8192, 192], P('tensor'), may hold values from -0.0625 to 0.0625
- unit_proj: bfloat16 [28672, 192], P(('tensor', 'dp')), may hold values from -0.03125 to 0.03125
- precond: float32 [3, 4096, 4096], P(None, ('tensor', 'dp')), may hold values from -20 to 20
Outputs:
- precond_grad: float32 [3, 8, 4096], P(None, 'groups', ('tensor', 'dp')), parts along dimension 1
There are 2 independent parts, one for each index of `groups`. A program takes and returns all parts, laid end to end along the dimension named above; an argument that names none is the same for every part. Nothing has to cross between parts.
All inputs are finite; a program needn't handle non-finite values.
Results may differ from a plain program's by a relative error of at most 0.0029.
Values may be sent and summed in bfloat16 or wider, within the bound.
No kernel may reach another device: no remote copies, remote signals or barrier semaphores. Data moves between devices by JAX's collectives and lax.ppermute only.
A program may use at most 256 MiB of HBM per device.

v0:
```python
import jax
import jax.numpy as jnp
from jax import lax
from jax.sharding import PartitionSpec as P

K = 64
SEQ = 128
contract_last = (((1,), (1,)), ((), ()))


def project_pair(rows_in, rows_out, columns):
    return jnp.concatenate(
        [
            jnp.dot(rows_in, columns[:, : 2 * K], preferred_element_type=jnp.float32),
            jnp.dot(rows_out, columns[:, 2 * K :], preferred_element_type=jnp.float32),
        ],
        axis=1,
    )


def form_sketch(in_side, out_side):
    seq_count = in_side.shape[0] // SEQ
    left_rows = in_side.reshape(seq_count, SEQ, 3, K)
    right_rows = out_side.reshape(seq_count, SEQ, 3, K)
    sketch = jnp.einsum("stwi,stwj->wsij", left_rows, right_rows, precision=lax.Precision.HIGHEST)
    sketch = sketch * SEQ ** (-0.5)
    return sketch.reshape(3, seq_count, K * K)


def local(hidden_in, out_grad, w_gate_up, w_down, feat_proj, unit_proj, precond):
    unit_width = w_down.shape[0]
    model_width = w_down.shape[1]
    w_both = w_gate_up.reshape(2 * unit_width, model_width)
    paired = jnp.stack([hidden_in, out_grad])
    tokens = hidden_in.shape[0] * lax.axis_size("dp")
    columns = lax.all_gather(feat_proj, "tensor", axis=0, tiled=True)
    feat_side = None
    rows_all = lax.all_gather(paired, "dp", axis=1, tiled=True)
    initial = [
        jnp.zeros((tokens, 2 * unit_width), jnp.float32),
        jnp.zeros((tokens, unit_width), jnp.float32),
    ]
    initial.append(jnp.zeros((tokens, 3 * K), jnp.float32))
    pieces = lax.all_gather(rows_all, "tensor", axis=2, tiled=True)
    result = [
        lax.dot_general(pieces[0], w_both, contract_last, preferred_element_type=jnp.float32),
        lax.dot_general(pieces[1], w_down, contract_last, preferred_element_type=jnp.float32),
    ]
    result.append(project_pair(pieces[0], pieces[1], columns))
    folded = tuple(result)
    pre_act = folded[0]
    hid_grad = folded[1]
    feat_side = folded[2]
    gate_pre = pre_act[:, :unit_width]
    up_pre = pre_act[:, unit_width:]
    gate_sig = jax.nn.sigmoid(gate_pre)
    silu_gate = gate_pre * gate_sig
    hidden = (silu_gate * up_pre).astype(jnp.bfloat16)
    gate_grad = (hid_grad * up_pre * gate_sig * (1.0 + gate_pre * (1.0 - gate_sig))).astype(
        jnp.bfloat16
    )
    up_grad = (hid_grad * silu_gate).astype(jnp.bfloat16)
    unit_part = jnp.concatenate(
        [
            jnp.dot(gate_grad, unit_proj[:, :K], preferred_element_type=jnp.float32),
            jnp.dot(up_grad, unit_proj[:, K : 2 * K], preferred_element_type=jnp.float32),
            jnp.dot(hidden, unit_proj[:, 2 * K :], preferred_element_type=jnp.float32),
        ],
        axis=1,
    )
    unit_side = lax.psum(unit_part, ("tensor", "dp"))
    in_side = jnp.concatenate([feat_side[:, : 2 * K], unit_side[:, 2 * K :]], axis=1)
    out_side = jnp.concatenate([unit_side[:, : 2 * K], feat_side[:, 2 * K :]], axis=1)
    sketch = form_sketch(in_side, out_side)
    return jnp.einsum("wrc,wsc->wsr", precond, sketch, precision=lax.Precision.HIGHEST)


def solution(mesh):
    in_specs = (
        P(("groups", "dp"), "tensor"),
        P(("groups", "dp"), "tensor"),
        P(None, ("tensor", "dp"), None),
        P(("tensor", "dp"), None),
        P("tensor", None),
        P(("tensor", "dp"), None),
        P(None, ("tensor", "dp"), None),
    )
    out_specs = P(None, "groups", ("tensor", "dp"))
    return jax.shard_map(local, mesh=mesh, in_specs=in_specs, out_specs=out_specs, check_vma=False)
```

profile of v0, /device:TPU:0, one launch (start us, length us, event | category | flops | bytes accessed | tf_op | source)
XLA Modules:
  0.0 386.8 jit_solution(336281864798562320)
XLA Ops:
  6.5 2.3 pad_maximum_fusion
  8.8 0.0 all-gather.6.cloned.1.call-start
  8.9 83.6 %all-gather.4.cloned.1.call-done = bf16[2,512,2048]{2,1,0:T(8,128)(2,1)} async-done(((bf16[2,128,2048]{2,1,0:T(8,128)(2,1)}), bf16[2,512,2048]{2,1,0:T(8,128)(2,1)}) %all-gather.4.cloned.1.call-update) | async-done | bytes 4194320 | tf_op jit(solution)/shard_map/all_gather | solution.py:38
  92.5 0.7 all-gather.8.cloned.1.call-update
  93.2 0.0 all-reduce.2.cloned.1.call-start
  93.3 105.2 %all-gather.6.cloned.1.call-done = bf16[2,512,8192]{2,1,0:T(8,128)(2,1)} async-done(((bf16[2,512,2048]{2,1,0:T(8,128)(2,1)}), bf16[2,512,8192]{2,1,0:T(8,128)(2,1)}) %all-gather.6.cloned.1.call-update) | async-done | bytes 16777232 | tf_op jit(solution)/shard_map/all_gather | solution.py:44
  198.5 38.6 %fusion = f32[512,3584]{1,0:T(8,128)} fusion(bf16[3584,8192]{1,0:T(8,128)(2,1)} %bitcast.23, bf16[2,512,8192]{2,1,0:T(8,128)(2,1)} %all-gather.6.cloned.1.call-done), kind=kOutput, calls=%fused_computation.2 | convolution fusion | flops 30064771072 | bytes 74448896 | tf_op jit(solution)/shard_map/dot_general | solution.py:46
  237.1 4.3 %fusion.7 = f32[512,64]{0,1:T(8,128)S(1)} fusion(f32[512,3584]{1,0:T(8,128)} %fusion, bf16[1792,192]{0,1:T(8,128)(2,1)S(1)} %copy-done), kind=kOutput, calls=%fused_computation.13 | convolution fusion | flops 122945536 | bytes 7700480 | tf_op jit(solution)/shard_map/dot_general | solution.py:67
  241.3 22.9 %fusion.3 = f32[512,1792]{1,0:T(8,128)} fusion(bf16[1792,8192]{1,0:T(8,128)(2,1)} %param.10, bf16[2,512,8192]{2,1,0:T(8,128)(2,1)} %all-gather.6.cloned.1.call-done), kind=kOutput, calls=%fused_computation.5 | convolution fusion | flops 15032385536 | bytes 41418752 | tf_op jit(solution)/shard_map/dot_general | solution.py:47
  264.3 4.4 %fusion.6 = f32[512,64]{0,1:T(8,128)S(1)} fusion(f32[512,1792]{1,0:T(8,128)} %fusion.3, f32[512,3584]{1,0:T(8,128)} %fusion, bf16[1792,192]{0,1:T(8,128)(2,1)S(1)} %copy-done), kind=kOutput, calls=%fused_computation.12 | convolution fusion | flops 122945536 | bytes 7700480 | tf_op jit(solution)/shard_map/dot_general | solution.py:66
  268.7 0.8 copy-done.1
  269.5 1.0 copy-done.2
  270.5 1.6 fusion.8
  272.1 0.8 pad_maximum_fusion.1
  272.9 6.9 %fusion.1 = f32[512,128]{0,1:T(8,128)S(1)} fusion(bf16[2,512,8192]{2,1,0:T(8,128)(2,1)} %all-gather.6.cloned.1.call-done, bf16[8192,192]{0,1:T(8,128)(2,1)} %all-gather.8.cloned.1.call-done), kind=kOutput, calls=%fused_computation.3 | convolution fusion | flops 1073741824 | bytes 10747904 | tf_op jit(solution)/shard_map/dot_general | solution.py:14
  279.8 6.3 %fusion.2 = f32[512,64]{0,1:T(8,128)S(1)} fusion(bf16[2,512,8192]{2,1,0:T(8,128)(2,1)} %all-gather.6.cloned.1.call-done, bf16[8192,192]{0,1:T(8,128)(2,1)} %all-gather.8.cloned.1.call-done), kind=kOutput, calls=%fused_computation.4 | convolution fusion | flops 536870912 | bytes 9568256 | tf_op jit(solution)/shard_map/dot_general | solution.py:15
  286.1 77.3 %all-reduce.2.cloned.1.call-done = f32[512,192]{0,1:T(8,128)} async-done(((f32[512,192]{0,1:T(8,128)}), f32[512,192]{0,1:T(8,128)}) %all-reduce.2.cloned.1.call-update) | async-done | bytes 393232 | tf_op jit(solution)/shard_map/psum | solution.py:71
  363.4 0.9 slice.51
  364.4 0.1 reshape.13
  364.5 1.0 slice.52
  365.5 0.1 reshape.14
  365.7 0.8 convolution_multiply_fusion
  366.4 0.2 reshape.15
  366.6 13.6 %fusion.20 = f32[3,4,256]{2,1,0:T(4,128)} fusion(f32[3,4,4096]{2,1,0:T(4,128)S(1)} %reshape.15, f32[3,256,4096]{2,1,0:T(8,128)} %param.13), kind=kOutput, calls=%fused_computation.29 | convolution fusion | flops 150994944 | bytes 12791808 | tf_op jit(solution)/shard_map/wrc,wsc->wsr/dot_general | solution.py:75
  (12 shorter events, 0.2 us)
Async XLA Ops:
  6.5 85.9 %all-gather.4.cloned.1.call-start = ((), (), s32[]{:S(2)}) async-start(), calls=%async_computation | async-start | bytes 5242880 | tf_op jit(solution)/shard_map/all_gather | solution.py:38
  8.8 189.7 %all-gather.6.cloned.1.call-start = ((), (), s32[]{:S(2)}) async-start(), calls=%async_computation.1 | async-start | bytes 20971520 | tf_op jit(solution)/shard_map/all_gather | solution.py:44
  92.5 180.4 %all-gather.8.cloned.1.call-start = ((), (), s32[]{:S(2)}) async-start(), calls=%async_computation.2 | async-start | bytes 3932160 | tf_op jit(solution)/shard_map/all_gather | solution.py:36
  93.2 270.2 %all-reduce.2.cloned.1.call-start = ((), (), s32[]{:S(2)}) async-start(), calls=%async_computation.3 | async-start | bytes 786432 | tf_op jit(solution)/shard_map/psum | solution.py:71
  198.5 38.6 %copy-start = (bf16[1792,192]{0,1:T(8,128)(2,1)S(1)}, bf16[1792,192]{0,1:T(8,128)(2,1)}, u32[]{:S(2)}) copy-start(bf16[1792,192]{0,1:T(8,128)(2,1)} %param.12) | copy-start | bytes 2064388
  264.3 5.2 %copy-start.1 = (f32[512,3584]{1,0:T(8,128)S(1)}, f32[512,3584]{1,0:T(8,128)}, u32[]{:S(2)}) copy-start(f32[512,3584]{1,0:T(8,128)} %fusion) | copy-start | bytes 22020100
  264.3 6.3 %copy-start.2 = (f32[512,1792]{1,0:T(8,128)S(1)}, f32[512,1792]{1,0:T(8,128)}, u32[]{:S(2)}) copy-start(f32[512,1792]{1,0:T(8,128)} %fusion.3) | copy-start | bytes 11010052
Sparse Core Ops, SparseCore 0:
  9.0 83.4 all-gather.3
  94.0 104.4 all-gather.5
  200.1 28.5 all-gather.7
  273.0 90.3 all-reduce.1
where the time goes:
time: 387 us
  waiting for transfers between devices  267 us (69%)
  matrix products  99.3 us (26%)
  between operations  13.2 us (3%)
  local copies, waits for them, and re-layouts  4.2 us (1%)
    all_gather x1, waiting for transfers between devices, local(): pieces = lax.all_gather(rows_all, 'tensor', axis=2, tiled=True)  105 us
    all_gather x1, waiting for transfers between devices, local(): rows_all = lax.all_gather(paired, 'dp', axis=1, tiled=True)  83.6 us
    psum x1, waiting for transfers between devices, local(): unit_side = lax.psum(unit_part, ('tensor', 'dp'))  77.3 us
    dot_general x1, matrix products, local(): lax.dot_general(pieces[0], w_both, contract_last, preferred_element_type=...  38.6 us
    dot_general x1, matrix products, local(): lax.dot_general(pieces[1], w_down, contract_last, preferred_element_type=...  22.9 us
    dot_general x1, matrix products, local(): jnp.einsum('wrc,wsc->wsr', precond, sketch, precision=lax.Precision.HIGHEST)  13.6 us
  transfers between devices with their start and end apart: 4, of which 3 were waited for; matrix products, arithmetic and copies ran while one was open for 22% of the time, Pallas kernels for 0%

commit v1 on v0

--- a/solution.py
+++ b/solution.py
@@ -6,6 +6,18 @@
 K = 64
 SEQ = 128
 contract_last = (((1,), (1,)), ((), ()))
+
+
+def doubled_up(array, axis, dim):
+    ways, here = (lax.axis_size(axis), lax.axis_index(axis))
+    grown, reach = (array, 1)
+    while reach < ways:
+        theirs = lax.ppermute(grown, axis, [(d, d ^ reach) for d in range(ways)])
+        mine_first = jnp.concatenate([grown, theirs], axis=dim)
+        theirs_first = jnp.concatenate([theirs, grown], axis=dim)
+        grown = jnp.where(here & reach == 0, mine_first, theirs_first)
+        reach = 2 * reach
+    return grown
 
 
 def project_pair(rows_in, rows_out, columns):
@@ -41,7 +53,7 @@
         jnp.zeros((tokens, unit_width), jnp.float32),
     ]
     initial.append(jnp.zeros((tokens, 3 * K), jnp.float32))
-    pieces = lax.all_gather(rows_all, "tensor", axis=2, tiled=True)
+    pieces = doubled_up(rows_all, "tensor", 2)
     result = [
         lax.dot_general(pieces[0], w_both, contract_last, preferred_element_type=jnp.float32),
         lax.dot_general(pieces[1], w_down, contract_last, preferred_element_type=jnp.float32),

time: 387 us -> 519 us (1.34)
  waiting for transfers between devices: 267 us -> 365 us
  other arithmetic: 3.1 us -> 33.6 us
    ppermute x0 -> x2, waiting for transfers between devices: none -> 206 us  [doubled_up(): theirs = lax.ppermute(grown, axis, [(d, d ^ reach) for d in range(ways)])]
    all_gather x1 -> x0, waiting for transfers between devices: 105 us -> none  [local(): pieces = lax.all_gather(rows_all, 'tensor', axis=2, tiled=True)]
    select_n x0 -> x2, other arithmetic: none -> 30.5 us  [doubled_up(): grown = jnp.where(here & reach == 0, mine_first, theirs_first)]
  transfers between devices with their start and end apart: 4 -> 5, of which waited for: 3 -> 4; matrix products, arithmetic and copies ran while one was open for 22% -> 20% of each run, Pallas kernels for 0% -> 0%
where the time goes in v1:
time: 519 us
  waiting for transfers between devices  365 us (70%)
  matrix products  99.3 us (19%)
  other arithmetic  33.6 us (6%)
  between operations  14.9 us (3%)
    ppermute x2, waiting for transfers between devices, doubled_up(): theirs = lax.ppermute(grown, axis, [(d, d ^ reach) for d in range(ways)])  206 us
    all_gather x1, waiting for transfers between devices, local(): rows_all = lax.all_gather(paired, 'dp', axis=1, tiled=True)  83.6 us
    psum x1, waiting for transfers between devices, local(): unit_side = lax.psum(unit_part, ('tensor', 'dp'))  75.8 us
    dot_general x1, matrix products, local(): lax.dot_general(pieces[0], w_both, contract_last, preferred_element_type=...  38.6 us
    select_n x2, other arithmetic, doubled_up(): grown = jnp.where(here & reach == 0, mine_first, theirs_first)  30.5 us
    dot_general x1, matrix products, local(): lax.dot_general(pieces[1], w_down, contract_last, preferred_element_type=...  22.9 us
    dot_general x1, matrix products, local(): jnp.einsum('wrc,wsc->wsr', precond, sketch, precision=lax.Precision.HIGHEST)  13.6 us
  transfers between devices with their start and end apart: 5, of which 4 were waited for; matrix products, arithmetic and copies ran while one was open for 20% of the time, Pallas kernels for 0%

profile of v1, /device:TPU:0, one launch (start us, length us, event | category | flops | bytes accessed | tf_op | source)
XLA Modules:
  0.0 518.6 jit_solution(16318961568072994263)
XLA Ops:
  7.4 2.3 pad_maximum_fusion
  9.7 83.6 %all-gather.3.cloned.1.call-done = bf16[2,512,2048]{2,1,0:T(8,128)(2,1)} async-done(((bf16[2,128,2048]{2,1,0:T(8,128)(2,1)}), bf16[2,512,2048]{2,1,0:T(8,128)(2,1)}) %all-gather.3.cloned.1.call-update) | async-done | bytes 4194320 | tf_op jit(solution)/shard_map/all_gather | solution.py:50
  93.3 7.5 %collective-permute-done = bf16[2,512,2048]{2,1,0:T(8,128)(2,1)} collective-permute-done((bf16[2,512,2048]{2,1,0:T(8,128)(2,1)}, bf16[2,512,2048]{2,1,0:T(8,128)(2,1)}, u32[]{:S(2)}, u32[]{:S(2)}) %collective-permute-start) | collective-permute-done | bytes 4194336 | tf_op jit(solution)/shard_map/ppermute | solution.py:15
  100.8 11.3 %maximum_select_fusion.1 = bf16[2,512,4096]{2,1,0:T(8,128)(2,1)} fusion(bf16[2,512,2048]{2,1,0:T(8,128)(2,1)} %collective-permute-done, bf16[2,512,2048]{2,1,0:T(8,128)(2,1)} %all-gather.3.cloned.1.call-done, pred[]{:T(512)S(6)} %eq.7), kind=kLoop, calls=%fused_computation.3 | loop fusion | flops 37748736 | bytes 16777216 | tf_op jit(solution)/shard_map/jit(_where)/select_n | solution.py:18
  112.1 1.5 collective-permute-start.1
  113.6 198.1 %collective-permute-done.1 = bf16[2,512,4096]{2,1,0:T(8,128)(2,1)} collective-permute-done((bf16[2,512,4096]{2,1,0:T(8,128)(2,1)}, bf16[2,512,4096]{2,1,0:T(8,128)(2,1)}, u32[]{:S(2)}, u32[]{:S(2)}) %collective-permute-start.1) | collective-permute-done | bytes 8388640 | tf_op jit(solution)/shard_map/ppermute | solution.py:15
  311.7 19.2 %maximum_select_fusion = bf16[2,512,8192]{2,1,0:T(8,128)(2,1)} fusion(bf16[2,512,4096]{2,1,0:T(8,128)(2,1)} %collective-permute-done.1, bf16[2,512,4096]{2,1,0:T(8,128)(2,1)} %maximum_select_fusion.1, pred[]{:T(512)S(6)} %eq.6), kind=kLoop, calls=%fused_computation | loop fusion | flops 75497472 | bytes 33554432 | tf_op jit(solution)/shard_map/jit(_where)/select_n | solution.py:18
  330.9 38.6 %fusion = f32[512,3584]{1,0:T(8,128)} fusion(bf16[3584,8192]{1,0:T(8,128)(2,1)} %bitcast.23, bf16[2,512,8192]{2,1,0:T(8,128)(2,1)} %maximum_select_fusion), kind=kOutput, calls=%fused_computation.4 | convolution fusion | flops 30064771072 | bytes 74448896 | tf_op jit(solution)/shard_map/dot_general | solution.py:58
  369.5 4.3 fusion.7
  373.8 22.9 %fusion.3 = f32[512,1792]{1,0:T(8,128)} fusion(bf16[1792,8192]{1,0:T(8,128)(2,1)} %param.10, bf16[2,512,8192]{2,1,0:T(8,128)(2,1)} %maximum_select_fusion), kind=kOutput, calls=%fused_computation.7 | convolution fusion | flops 15032385536 | bytes 41418752 | tf_op jit(solution)/shard_map/dot_general | solution.py:59
  396.7 4.4 fusion.6
  401.1 0.8 copy-done.1
  401.9 1.0 copy-done.2
  402.9 1.6 fusion.8
  404.5 0.8 pad_maximum_fusion.1
  405.3 6.9 %fusion.1 = f32[512,128]{0,1:T(8,128)S(1)} fusion(bf16[2,512,8192]{2,1,0:T(8,128)(2,1)} %maximum_select_fusion, bf16[8192,192]{0,1:T(8,128)(2,1)} %all-gather.5.cloned.1.call-done), kind=kOutput, calls=%fused_computation.5 | convolution fusion | flops 1073741824 | bytes 10747904 | tf_op jit(solution)/shard_map/dot_general | solution.py:26
  412.2 6.3 %fusion.2 = f32[512,64]{0,1:T(8,128)S(1)} fusion(bf16[2,512,8192]{2,1,0:T(8,128)(2,1)} %maximum_select_fusion, bf16[8192,192]{0,1:T(8,128)(2,1)} %all-gather.5.cloned.1.call-done), kind=kOutput, calls=%fused_computation.6 | convolution fusion | flops 536870912 | bytes 9568256 | tf_op jit(solution)/shard_map/dot_general | solution.py:27
  418.5 75.8 %all-reduce.2.cloned.1.call-done = f32[512,192]{0,1:T(8,128)} async-done(((f32[512,192]{0,1:T(8,128)}), f32[512,192]{0,1:T(8,128)}) %all-reduce.2.cloned.1.call-update) | async-done | bytes 393232 | tf_op jit(solution)/shard_map/psum | solution.py:83
  494.4 0.9 slice.51
  495.3 0.1 reshape.13
  495.5 1.0 slice.52
  496.6 0.7 convolution_multiply_fusion
  497.4 0.2 reshape.15
  497.6 13.6 %fusion.20 = f32[3,4,256]{2,1,0:T(4,128)} fusion(f32[3,4,4096]{2,1,0:T(4,128)S(1)} %reshape.15, f32[3,256,4096]{2,1,0:T(8,128)} %param.13), kind=kOutput, calls=%fused_computation.31 | convolution fusion | flops 150994944 | bytes 12791808 | tf_op jit(solution)/shard_map/wrc,wsc->wsr/dot_general | solution.py:87
  (15 shorter events, 0.4 us)
Async XLA Ops:
  7.4 85.9 %all-gather.3.cloned.1.call-start = ((), (), s32[]{:S(2)}) async-start(), calls=%async_computation | async-start | bytes 5242880 | tf_op jit(solution)/shard_map/all_gather | solution.py:50
  9.7 395.7 %all-gather.5.cloned.1.call-start = ((), (), s32[]{:S(2)}) async-start(), calls=%async_computation.1 | async-start | bytes 3932160 | tf_op jit(solution)/shard_map/all_gather | solution.py:48
  93.3 7.5 %collective-permute-start = (bf16[2,512,2048]{2,1,0:T(8,128)(2,1)}, bf16[2,512,2048]{2,1,0:T(8,128)(2,1)}, u32[]{:S(2)}, u32[]{:S(2)}) collective-permute-start(bf16[2,512,2048]{2,1,0:T(8,128)(2,1)} %all-gather.3.cloned.1.call-done), channel_id=1, source_target_pairs={{0,4},{4,0},{8,12},{12,8},{1,5},{5,1},{9,13},{13,9},{2,6},{6,2},{1... | collective-permute-start | bytes 12582920 | tf_op jit(solution)/shard_map/ppermute | solution.py:15
  112.1 199.7 %collective-permute-start.1 = (bf16[2,512,4096]{2,1,0:T(8,128)(2,1)}, bf16[2,512,4096]{2,1,0:T(8,128)(2,1)}, u32[]{:S(2)}, u32[]{:S(2)}) collective-permute-start(bf16[2,512,4096]{2,1,0:T(8,128)(2,1)} %maximum_select_fusion.1), channel_id=1, source_target_pairs={{0,8},{4,12},{8,0},{12,4},{1,9},{5,13},{9,1},{13,5},{2,10},{6,14},... | collective-permute-start | bytes 25165832 | tf_op jit(solution)/shard_map/ppermute | solution.py:15
  113.6 380.8 %all-reduce.2.cloned.1.call-start = ((), (), s32[]{:S(2)}) async-start(), calls=%async_computation.2 | async-start | bytes 786432 | tf_op jit(solution)/shard_map/psum | solution.py:83
  330.9 38.6 %copy-start = (bf16[1792,192]{0,1:T(8,128)(2,1)S(1)}, bf16[1792,192]{0,1:T(8,128)(2,1)}, u32[]{:S(2)}) copy-start(bf16[1792,192]{0,1:T(8,128)(2,1)} %param.12) | copy-start | bytes 2064388
  396.7 5.2 %copy-start.1 = (f32[512,3584]{1,0:T(8,128)S(1)}, f32[512,3584]{1,0:T(8,128)}, u32[]{:S(2)}) copy-start(f32[512,3584]{1,0:T(8,128)} %fusion) | copy-start | bytes 22020100
  396.7 6.3 %copy-start.2 = (f32[512,1792]{1,0:T(8,128)S(1)}, f32[512,1792]{1,0:T(8,128)}, u32[]{:S(2)}) copy-start(f32[512,1792]{1,0:T(8,128)} %fusion.3) | copy-start | bytes 11010052
Sparse Core Ops, SparseCore 0:
  9.8 83.4 all-gather.2
  405.4 88.8 all-reduce.1
Sparse Core Ops, SparseCore 1:
  113.6 42.9 all-gather.4
